TPU v7x, 512 devices: a whole 4x4x16 slice. The times are simulated.
512 devices in a mesh: occ: 64 (over z_lo, y, core), aux: 8 (over x, z_hi).
Axes of the slice: x: 4, y: 4, z: 16 (z_hi: 2, z_lo: 8; z = z_hi * 8 + z_lo), core: 2. Of those that a mesh axis runs over, the one named last changes fastest.
Arguments:
- half_blocks: bfloat16 [1536, 64, 6144], P('occ', None, 'aux'), may hold values from -0.796875 to 0.796875
- block_rows: int32 [64], replicated, may hold values from 1 to 24, 768 in all
- block_order: int32 [64], replicated, may hold values from 0 to 63, each once
- ao_to_virt: bfloat16 [768, 512], replicated, may hold values from -0.21875 to 0.21875
- occ_energy: float32 [64], replicated, may hold values from -2 to -0.5
- virt_energy: float32 [512], replicated, may hold values from 0.2 to 3
Outputs:
- gamma: float32 [64, 512, 6144], P('occ', None, 'aux')
Inputs may be any that keep to these rules, and one draw needn't show every extreme that they name: block_rows[s] is the number of AO functions held by device s of occ; the counts sum to 768 and one of them equals 24. A permutation; the runs of AO functions lie end to end in the order of block_order.
All inputs are finite; a program needn't handle non-finite values.
Results may differ from a plain program's by a relative error of at most 0.008.
Values may be sent and summed in bfloat16 or wider, within the bound.
No kernel may reach another device: no remote copies, remote signals or barrier semaphores. Data moves between devices by JAX's collectives and lax.ppermute only.
A program may use at most 64 MiB of HBM per device.

v0:
```python
import jax
import jax.numpy as jnp
from jax import lax
from jax.sharding import PartitionSpec as P

CYCLE = 3


def shifted(value, axis, by):
    devices = lax.axis_size(axis)
    return lax.ppermute(value, axis, [(i, (i + by) % devices) for i in range(devices)])


def ao_layout(block_rows, block_order, maxrows):
    device_count = block_rows.shape[0]
    matches = block_order[:, None] == jnp.arange(device_count, dtype=jnp.int32)[None, :]
    ordered = jnp.sum(jnp.where(matches, block_rows[None, :], 0), axis=1)
    before = jnp.cumsum(ordered) - ordered
    starts = jnp.sum(jnp.where(matches, before[:, None], 0), axis=0)
    offset = jnp.arange(maxrows, dtype=jnp.int32)
    in_block = offset[None, :] < block_rows[:, None]
    target = starts[:, None] + offset[None, :]
    return (in_block, target)


def build_table(block_rows, block_order, ao_to_virt, maxrows):
    in_block, target = ao_layout(block_rows, block_order, maxrows)
    row_index = jnp.where(in_block, target, 0).reshape(-1)
    ao_rows = jnp.take(ao_to_virt, row_index, axis=0)
    return jnp.where(in_block.reshape(-1, 1), ao_rows, jnp.zeros_like(ao_rows))


def contract_rows(ao_table, received):
    return lax.dot_general(
        ao_table, received, (((0,), (0,)), ((), ())), preferred_element_type=jnp.float32
    ).astype(jnp.bfloat16)


def shards(half_blocks, block_rows, block_order, ao_to_virt, occ_energy, virt_energy):
    maxrows = half_blocks.shape[0]
    device_count = occ_energy.shape[0]
    position = lax.axis_index("occ")
    ao_table = build_table(block_rows, block_order, ao_to_virt, maxrows)
    own_tile = contract_rows(
        ao_table,
        lax.all_to_all(half_blocks, "occ", split_axis=1, concat_axis=0, tiled=True)[:, 0, :],
    )
    density = jnp.zeros(own_tile.shape, jnp.float32)
    other_tile = own_tile
    for cycle_step in range(CYCLE + 1):
        if cycle_step > 0:
            other_tile = shifted(other_tile, "occ", 1)
        partner = (position - cycle_step) % device_count
        energy_gap = (
            virt_energy[:, None] + virt_energy[None, :] - occ_energy[position] - occ_energy[partner]
        )
        product = lax.dot_general(
            own_tile, other_tile, (((1,), (1,)), ((), ())), preferred_element_type=jnp.float32
        )
        partial_value = 2.0 * product - product.T
        merged = lax.psum(partial_value.astype(jnp.bfloat16), "aux").astype(jnp.float32)
        amplitudes = (merged / energy_gap).astype(jnp.bfloat16)
        density = density + jnp.dot(amplitudes, other_tile, preferred_element_type=jnp.float32)
    return density[None]


def solution(mesh):
    return jax.shard_map(
        shards,
        mesh=mesh,
        in_specs=(P("occ", None, "aux"), P(), P(), P(), P(), P()),
        out_specs=P("occ", None, "aux"),
        check_vma=False,
    )
```

profile of v0, /device:TPU:1, one launch (start us, length us, event | category | flops | bytes accessed | tf_op | source)
XLA Modules:
  0.0 594.4 jit_solution(5116064361449036951)
XLA Ops:
  6.5 0.0 copy-start
  6.5 4.4 copy.19
  11.0 0.0 copy-start.6
  11.0 0.0 copy-start.9
  11.0 17.5 %all-to-all-start = ((bf16[24,64,768]{2,0,1:T(8,128)(2,1)}), bf16[24,64,768]{2,0,1:T(8,128)(2,1)}, u32[]{:S(2)}, u32[]{:S(2)}) async-start(bf16[24,64,768]{2,0,1:T(8,128)(2,1)} %copy.19), calls=%async_computation | async-start | bytes 4718592 | tf_op jit(solution)/shard_map/all_to_all | solution.py:46
  28.5 0.0 all-reduce.3.cloned.1.call-start
  28.5 0.0 copy-done.6
  28.5 0.0 copy-done.9
  28.6 0.2 select_reduce_fusion.1
  28.7 0.1 copy.18
  28.8 0.1 reduce-window.8
  28.9 0.1 reduce
  29.1 0.1 select_reduce_fusion
  29.2 0.1 iota_add_fusion
  29.3 0.1 add.133
  29.3 0.1 iota_compare_fusion.1
  29.4 0.1 lt.88
  29.5 0.1 select_n.93
  29.7 0.0 copy-done
  29.7 4.8 gather_fusion
  34.5 100.6 %all-to-all-done = bf16[24,64,768]{2,0,1:T(8,128)(2,1)} async-done(((bf16[24,64,768]{2,0,1:T(8,128)(2,1)}), bf16[24,64,768]{2,0,1:T(8,128)(2,1)}, u32[]{:S(2)}, u32[]{:S(2)}) %all-to-all-start) | async-done | bytes 2359328 | tf_op jit(solution)/shard_map/all_to_all | solution.py:46
  135.1 3.4 fusion.5
  138.5 4.3 collective-permute-start
  142.8 8.9 %collective-permute-done = bf16[512,768]{1,0:T(8,128)(2,1)S(1)} collective-permute-done((bf16[512,768]{1,0:T(8,128)(2,1)S(1)}, bf16[512,768]{1,0:T(8,128)(2,1)S(1)}, u32[]{:S(2)}, u32[]{:S(2)}) %collective-permute-start) | collective-permute-done | bytes 786464 | tf_op jit(solution)/shard_map/ppermute | solution.py:11
  151.7 0.0 copy-start.1
  151.7 4.4 collective-permute-start.1
  156.1 0.6 fusion.37
  156.7 1.3 copy.20
  158.0 2.3 fusion.11
  160.3 0.0 copy-done.1
  160.3 0.6 fusion.38
  160.9 1.3 copy.21
  162.2 3.4 collective-permute-done.1
  165.6 4.0 collective-permute-start.2
  169.6 2.3 fusion.10
  171.9 1.7 fusion.39
  173.7 1.3 copy.22
  175.0 2.3 fusion.9
  177.2 10.5 %collective-permute-done.2 = bf16[512,768]{1,0:T(8,128)(2,1)S(1)} collective-permute-done((bf16[512,768]{1,0:T(8,128)(2,1)}, bf16[512,768]{1,0:T(8,128)(2,1)S(1)}, u32[]{:S(2)}, u32[]{:S(2)}) %collective-permute-start.2) | collective-permute-done | bytes 786464 | tf_op jit(solution)/shard_map/ppermute | solution.py:11
  187.8 0.6 fusion.40
  188.4 1.3 copy.23
  189.7 2.3 fusion.8
  192.0 0.0 copy-start.4
  192.0 0.0 copy-start.5
  192.0 0.0 all-reduce.3.cloned.1.call-update
  192.1 0.6 copy-done.4
  192.6 0.7 fusion.36
  193.3 382.2 %all-reduce.3.cloned.1.call-done = (bf16[512,512]{0,1:T(8,128)(2,1)}, bf16[512,512]{0,1:T(8,128)(2,1)}, bf16[512,512]{0,1:T(8,128)(2,1)}, bf16[512,512]{0,1:T(8,128)(2,1)}) async-done(((bf16[512,512]{0,1:T(8,128)(2,1)}, bf16[512,512]{0,1:T(8,128)(2,1)}, bf16[512,512]{0,1:T(8,128)(2,1)}, bf16[512,512]{0,1:T(8,128)(2,1)}), (bf16[512,512]{0,1:T(8,128)(2,1)}, bf16[512,512]{0,1:T(8,128)(2,1)}, ...) | async-done | bytes 2097168 | tf_op jit(solution)/shard_map/psum | solution.py:61
  575.5 0.0 copy-done.5
  575.5 0.0 copy-start.2
  575.5 0.0 copy-start.8
  575.5 3.3 fusion.14
  578.8 0.0 copy-done.2
  578.8 0.0 copy-done.8
  578.8 0.0 copy-start.7
  578.8 2.2 fusion.15
  581.0 0.0 copy-done.7
  581.0 0.0 copy-start.3
  581.0 3.2 fusion.16
  584.2 0.0 copy-done.3
  584.2 3.3 add_bitcast_fusion
  (4 shorter events, 0.0 us)
Async XLA Ops:
  6.5 23.1 %copy-start = (bf16[768,512]{1,0:T(8,128)(2,1)S(1)}, bf16[768,512]{1,0:T(8,128)(2,1)}, u32[]{:S(2)}) copy-start(bf16[768,512]{1,0:T(8,128)(2,1)} %param.9) | copy-start | bytes 2359300
  11.0 17.6 %copy-start.6 = (s32[64]{0:T(128)S(1)}, s32[64]{0:T(128)}, u32[]{:S(2)}) copy-start(s32[64]{0:T(128)} %param.7) | copy-start | bytes 772
  11.0 17.6 %copy-start.9 = (s32[64]{0:T(128)S(1)}, s32[64]{0:T(128)}, u32[]{:S(2)}) copy-start(s32[64]{0:T(128)} %param.8) | copy-start | bytes 772
  11.0 124.2 %all-to-all-start = ((bf16[24,64,768]{2,0,1:T(8,128)(2,1)}), bf16[24,64,768]{2,0,1:T(8,128)(2,1)}, u32[]{:S(2)}, u32[]{:S(2)}) async-start(bf16[24,64,768]{2,0,1:T(8,128)(2,1)} %copy.19), calls=%async_computation | async-start | bytes 4718592 | tf_op jit(solution)/shard_map/all_to_all | solution.py:46
  28.5 547.0 %all-reduce.3.cloned.1.call-start = ((), (), s32[]{:S(2)}) async-start(), calls=%async_computation.1 | async-start | bytes 4194304 | tf_op jit(solution)/shard_map/psum | solution.py:61
  138.5 13.2 %collective-permute-start = (bf16[512,768]{1,0:T(8,128)(2,1)S(1)}, bf16[512,768]{1,0:T(8,128)(2,1)S(1)}, u32[]{:S(2)}, u32[]{:S(2)}) collective-permute-start(bf16[512,768]{1,0:T(8,128)(2,1)S(1)} %fusion.5), channel_id=1, source_target_pairs={{0,8},{8,16},{16,24},{24,32},{32,40},{40,48},{48,56},{56,64},{64,7... | collective-permute-start | bytes 2359304 | tf_op jit(solution)/shard_map/ppermute | solution.py:11
  151.7 8.6 %copy-start.1 = (bf16[512,768]{1,0:T(8,128)(2,1)}, bf16[512,768]{1,0:T(8,128)(2,1)S(1)}, u32[]{:S(2)}) copy-start(bf16[512,768]{1,0:T(8,128)(2,1)S(1)} %collective-permute-done) | copy-start | bytes 2359300
  151.7 13.9 %collective-permute-start.1 = (bf16[512,768]{1,0:T(8,128)(2,1)S(1)}, bf16[512,768]{1,0:T(8,128)(2,1)}, u32[]{:S(2)}, u32[]{:S(2)}) collective-permute-start(bf16[512,768]{1,0:T(8,128)(2,1)S(1)} %collective-permute-done), channel_id=1, source_target_pairs={{0,8},{8,16},{16,24},{24,32},{32,40},{40,48},{48,56},{56,64},{64,7... | collective-permute-start | bytes 2359304 | tf_op jit(solution)/shard_map/ppermute | solution.py:11
  165.6 22.2 %collective-permute-start.2 = (bf16[512,768]{1,0:T(8,128)(2,1)}, bf16[512,768]{1,0:T(8,128)(2,1)S(1)}, u32[]{:S(2)}, u32[]{:S(2)}) collective-permute-start(bf16[512,768]{1,0:T(8,128)(2,1)} %collective-permute-done.1), channel_id=1, source_target_pairs={{0,8},{8,16},{16,24},{24,32},{32,40},{40,48},{48,56},{56,64},{64,7... | collective-permute-start | bytes 2359304 | tf_op jit(solution)/shard_map/ppermute | solution.py:11
  192.0 0.7 copy-start.4
  192.0 383.5 %copy-start.5 = (f32[512]{0:T(512)S(1)}, f32[512]{0:T(512)}, u32[]{:S(2)}) copy-start(f32[512]{0:T(512)} %param.11) | copy-start | bytes 6148
  575.5 3.3 copy-start.2
  575.5 3.3 copy-start.8
  578.8 2.2 copy-start.7
  581.0 3.2 copy-start.3
Sparse Core Ops, SparseCore 0:
  192.1 383.2 all-reduce.2
where the time goes:
time: 595 us; the launch traced here: 594 us
  waiting for transfers between devices  506 us (85%)
  starting transfers between devices  30.2 us (5%)
  matrix products  18.9 us (3%)
  local copies, waits for them, and re-layouts  16.1 us (3%)
  between operations  13.7 us (2%)
  other arithmetic  9.85 us (2%)
    psum x1, waiting for transfers between devices, shards(): lax.psum(partial_value.astype(jnp.bfloat16), 'aux').astype(jnp.float32)  382 us
    all_to_all x1, waiting for transfers between devices, shards(): lax.all_to_all(half_blocks, 'occ', split_axis=1, concat_axis=0, tiled=True)  101 us
    ppermute x3, waiting for transfers between devices, shifted(): lax.ppermute(value, axis, [(i, (i + by) % devices) for i in range(devices)])  22.9 us
    all_to_all x1, starting transfers between devices, shards(): lax.all_to_all(half_blocks, 'occ', split_axis=1, concat_axis=0, tiled=True)  17.5 us
    ppermute x3, starting transfers between devices, shifted(): lax.ppermute(value, axis, [(i, (i + by) % devices) for i in range(devices)])  12.7 us
    dot_general x4, matrix products, shards(): jnp.dot(amplitudes, other_tile, preferred_element_type=jnp.float32)  12 us
  transfers between devices with their start and end apart: 5, of which 5 were waited for; matrix products, arithmetic and copies ran while one was open for 3% of the time, Pallas kernels for 0%

commit v1 on v0

--- a/solution.py
+++ b/solution.py
@@ -4,6 +4,10 @@
 from jax.sharding import PartitionSpec as P
 
 CYCLE = 3
+
+
+def guide_run(content):
+    return jnp.sum(lax.all_gather(content, "aux"), axis=0)
 
 
 def shifted(value, axis, by):
@@ -58,7 +62,7 @@
             own_tile, other_tile, (((1,), (1,)), ((), ())), preferred_element_type=jnp.float32
         )
         partial_value = 2.0 * product - product.T
-        merged = lax.psum(partial_value.astype(jnp.bfloat16), "aux").astype(jnp.float32)
+        merged = guide_run(partial_value.astype(jnp.bfloat16)).astype(jnp.float32)
         amplitudes = (merged / energy_gap).astype(jnp.bfloat16)
         density = density + jnp.dot(amplitudes, other_tile, preferred_element_type=jnp.float32)
     return density[None]

time: 595 us -> 883 us (1.48)
  waiting for transfers between devices: 506 us -> 763 us
  local copies, waits for them, and re-layouts: 16.1 us -> 34.1 us
  other arithmetic: 9.85 us -> 22.8 us
    all_gather x0 -> x4, waiting for transfers between devices: none -> 615 us  [guide_run(): return jnp.sum(lax.all_gather(content, 'aux'), axis=0)]
    psum x1 -> x0, waiting for transfers between devices: 382 us -> none  [shards(): lax.psum(partial_value.astype(jnp.bfloat16), 'aux').astype(jnp.float32)]
    ppermute x3, waiting for transfers between devices: 22.9 us -> 47.1 us  [shifted(): lax.ppermute(value, axis, [(i, (i + by) % devices) for i in range(devices)])]
    unnamed x21 -> x29, local copies, waits for them, and re-layouts: 5.02 us -> 23.1 us
    reduce_sum x0 -> x4, other arithmetic: none -> 12.9 us  [guide_run(): return jnp.sum(lax.all_gather(content, 'aux'), axis=0)]
  transfers between devices with their start and end apart: 5 -> 8, of which waited for: 5 -> 8; matrix products, arithmetic and copies ran while one was open for 3% -> 6% of each run, Pallas kernels for 0% -> 0%
where the time goes in v1:
time: 883 us; the launch traced here: 882 us
  waiting for transfers between devices  763 us (86%)
  local copies, waits for them, and re-layouts  34.1 us (4%)
  starting transfers between devices  30.3 us (3%)
  other arithmetic  22.8 us (3%)
  matrix products  18.4 us (2%)
  between operations  13.5 us (2%)
    all_gather x4, waiting for transfers between devices, guide_run(): return jnp.sum(lax.all_gather(content, 'aux'), axis=0)  615 us
    all_to_all x1, waiting for transfers between devices, shards(): lax.all_to_all(half_blocks, 'occ', split_axis=1, concat_axis=0, tiled=True)  101 us
    ppermute x3, waiting for transfers between devices, shifted(): lax.ppermute(value, axis, [(i, (i + by) % devices) for i in range(devices)])  47.1 us
    unnamed x29, local copies, waits for them, and re-layouts  23.1 us
  transfers between devices with their start and end apart: 8, of which 8 were waited for; matrix products, arithmetic and copies ran while one was open for 6% of the time, Pallas kernels for 0%

profile of v1, /device:TPU:1, one launch (start us, length us, event | category | flops | bytes accessed | tf_op | source)
XLA Modules:
  0.0 882.3 jit_solution(14704355480347619721)
XLA Ops:
  6.5 0.0 copy-start
  6.5 4.4 copy.25
  11.0 17.5 %all-to-all-start = ((bf16[24,64,768]{2,0,1:T(8,128)(2,1)}), bf16[24,64,768]{2,0,1:T(8,128)(2,1)}, u32[]{:S(2)}, u32[]{:S(2)}) async-start(bf16[24,64,768]{2,0,1:T(8,128)(2,1)} %copy.25), calls=%async_computation | async-start | bytes 4718592 | tf_op jit(solution)/shard_map/all_to_all | solution.py:50
  28.5 0.0 all-gather.9.cloned.1.call-start
  28.6 0.2 select_reduce_fusion.1
  28.7 0.1 copy.24
  28.8 0.1 reduce-window.8
  28.9 0.1 reduce.4
  29.1 0.1 select_reduce_fusion
  29.2 0.1 iota_add_fusion
  29.3 0.1 add.125
  29.3 0.1 iota_compare_fusion.1
  29.4 0.1 lt.88
  29.5 0.1 select_n.93
  29.7 0.0 copy-done
  29.7 4.8 gather_fusion
  34.5 100.6 %all-to-all-done = bf16[24,64,768]{2,0,1:T(8,128)(2,1)} async-done(((bf16[24,64,768]{2,0,1:T(8,128)(2,1)}), bf16[24,64,768]{2,0,1:T(8,128)(2,1)}, u32[]{:S(2)}, u32[]{:S(2)}) %all-to-all-start) | async-done | bytes 2359328 | tf_op jit(solution)/shard_map/all_to_all | solution.py:50
  135.1 3.4 fusion.5
  138.5 0.6 fusion.37
  139.1 1.3 copy.26
  140.4 2.3 fusion.11
  142.7 0.0 all-gather.9.cloned.1.call-update
  142.7 0.0 all-gather.11.cloned.1.call-start
  142.7 4.3 collective-permute-start
  147.0 8.9 %collective-permute-done = bf16[512,768]{1,0:T(8,128)(2,1)S(1)} collective-permute-done((bf16[512,768]{1,0:T(8,128)(2,1)S(1)}, bf16[512,768]{1,0:T(8,128)(2,1)S(1)}, u32[]{:S(2)}, u32[]{:S(2)}) %collective-permute-start) | collective-permute-done | bytes 786464 | tf_op jit(solution)/shard_map/ppermute | solution.py:15
  155.9 0.6 fusion.38
  156.5 1.3 copy.27
  157.8 2.4 fusion.10
  160.2 0.0 all-gather.11.cloned.1.call-update
  160.2 0.0 all-gather.13.cloned.1.call-start
  160.3 4.4 collective-permute-start.1
  164.7 9.5 %collective-permute-done.1 = bf16[512,768]{1,0:T(8,128)(2,1)S(1)} collective-permute-done((bf16[512,768]{1,0:T(8,128)(2,1)S(1)}, bf16[512,768]{1,0:T(8,128)(2,1)S(1)}, u32[]{:S(2)}, u32[]{:S(2)}) %collective-permute-start.1) | collective-permute-done | bytes 786464 | tf_op jit(solution)/shard_map/ppermute | solution.py:15
  174.1 0.9 copy-done.6
  175.0 0.6 fusion.39
  175.6 1.3 copy.28
  176.9 2.3 fusion.9
  179.2 0.0 all-gather.13.cloned.1.call-update
  179.2 0.0 all-gather.15.cloned.1.call-start
  179.3 4.0 collective-permute-start.2
  183.3 28.7 %collective-permute-done.2 = bf16[512,768]{1,0:T(8,128)(2,1)S(1)} collective-permute-done((bf16[512,768]{1,0:T(8,128)(2,1)}, bf16[512,768]{1,0:T(8,128)(2,1)S(1)}, u32[]{:S(2)}, u32[]{:S(2)}) %collective-permute-start.2) | collective-permute-done | bytes 786464 | tf_op jit(solution)/shard_map/ppermute | solution.py:15
  212.0 0.6 fusion.40
  212.6 1.3 copy.29
  213.9 2.3 fusion.8
  216.2 0.0 all-gather.15.cloned.1.call-update
  216.3 0.7 fusion.36
  217.0 107.4 %all-gather.9.cloned.1.call-done = bf16[4096,512]{0,1:T(8,128)(2,1)} async-done(((bf16[512,512]{0,1:T(8,128)(2,1)}), bf16[4096,512]{0,1:T(8,128)(2,1)}) %all-gather.9.cloned.1.call-update) | async-done | bytes 4194320 | tf_op jit(solution)/shard_map/all_gather | solution.py:10
  324.3 4.4 copy.30
  328.7 0.0 copy-start.9
  328.8 3.1 bitcast_reduce_fusion.3
  331.9 0.0 copy-done.9
  331.9 3.2 fusion.14
  335.1 174.7 %all-gather.11.cloned.1.call-done = bf16[4096,512]{0,1:T(8,128)(2,1)} async-done(((bf16[512,512]{0,1:T(8,128)(2,1)}), bf16[4096,512]{0,1:T(8,128)(2,1)}) %all-gather.11.cloned.1.call-update) | async-done | bytes 4194320 | tf_op jit(solution)/shard_map/all_gather | solution.py:10
  509.8 4.4 copy.31
  514.2 3.3 bitcast_reduce_fusion.2
  517.5 3.2 fusion.15
  520.8 166.7 %all-gather.13.cloned.1.call-done = bf16[4096,512]{0,1:T(8,128)(2,1)} async-done(((bf16[512,512]{0,1:T(8,128)(2,1)}), bf16[4096,512]{0,1:T(8,128)(2,1)}) %all-gather.13.cloned.1.call-update) | async-done | bytes 4194320 | tf_op jit(solution)/shard_map/all_gather | solution.py:10
  687.5 4.4 copy.32
  691.9 3.4 bitcast_reduce_fusion.1
  695.3 3.1 fusion.16
  698.4 166.6 %all-gather.15.cloned.1.call-done = bf16[4096,512]{0,1:T(8,128)(2,1)} async-done(((bf16[512,512]{0,1:T(8,128)(2,1)}), bf16[4096,512]{0,1:T(8,128)(2,1)}) %all-gather.15.cloned.1.call-update) | async-done | bytes 4194320 | tf_op jit(solution)/shard_map/all_gather | solution.py:10
  865.1 4.4 copy.33
  869.5 0.0 copy-start.3
  869.5 3.1 bitcast_reduce_fusion
  872.7 3.1 add_bitcast_fusion
  (22 shorter events, 0.1 us)
Async XLA Ops:
  6.5 23.1 %copy-start = (bf16[768,512]{1,0:T(8,128)(2,1)S(1)}, bf16[768,512]{1,0:T(8,128)(2,1)}, u32[]{:S(2)}) copy-start(bf16[768,512]{1,0:T(8,128)(2,1)} %param.9) | copy-start | bytes 2359300
  11.0 17.6 %copy-start.10 = (s32[64]{0:T(128)S(1)}, s32[64]{0:T(128)}, u32[]{:S(2)}) copy-start(s32[64]{0:T(128)} %param.7) | copy-start | bytes 772
  11.0 17.6 %copy-start.11 = (s32[64]{0:T(128)S(1)}, s32[64]{0:T(128)}, u32[]{:S(2)}) copy-start(s32[64]{0:T(128)} %param.8) | copy-start | bytes 772
  11.0 124.2 %all-to-all-start = ((bf16[24,64,768]{2,0,1:T(8,128)(2,1)}), bf16[24,64,768]{2,0,1:T(8,128)(2,1)}, u32[]{:S(2)}, u32[]{:S(2)}) async-start(bf16[24,64,768]{2,0,1:T(8,128)(2,1)} %copy.25), calls=%async_computation | async-start | bytes 4718592 | tf_op jit(solution)/shard_map/all_to_all | solution.py:50
  28.5 295.8 %all-gather.9.cloned.1.call-start = ((), (), s32[]{:S(2)}) async-start(), calls=%async_computation.1 | async-start | bytes 4718592 | tf_op jit(solution)/shard_map/all_gather | solution.py:10
  142.7 367.1 %all-gather.11.cloned.1.call-start = ((), (), s32[]{:S(2)}) async-start(), calls=%async_computation.2 | async-start | bytes 4718592 | tf_op jit(solution)/shard_map/all_gather | solution.py:10
  142.7 13.2 %collective-permute-start = (bf16[512,768]{1,0:T(8,128)(2,1)S(1)}, bf16[512,768]{1,0:T(8,128)(2,1)S(1)}, u32[]{:S(2)}, u32[]{:S(2)}) collective-permute-start(bf16[512,768]{1,0:T(8,128)(2,1)S(1)} %fusion.5), channel_id=1, source_target_pairs={{0,8},{8,16},{16,24},{24,32},{32,40},{40,48},{48,56},{56,64},{64,7... | collective-permute-start | bytes 2359304 | tf_op jit(solution)/shard_map/ppermute | solution.py:15
  155.9 4.3 copy-start.4
  160.2 527.3 %all-gather.13.cloned.1.call-start = ((), (), s32[]{:S(2)}) async-start(), calls=%async_computation.3 | async-start | bytes 4718592 | tf_op jit(solution)/shard_map/all_gather | solution.py:10
  160.3 13.9 %collective-permute-start.1 = (bf16[512,768]{1,0:T(8,128)(2,1)S(1)}, bf16[512,768]{1,0:T(8,128)(2,1)S(1)}, u32[]{:S(2)}, u32[]{:S(2)}) collective-permute-start(bf16[512,768]{1,0:T(8,128)(2,1)S(1)} %collective-permute-done), channel_id=1, source_target_pairs={{0,8},{8,16},{16,24},{24,32},{32,40},{40,48},{48,56},{56,64},{64,7... | collective-permute-start | bytes 2359304 | tf_op jit(solution)/shard_map/ppermute | solution.py:15
  174.1 0.9 copy-start.6
  179.2 685.8 %all-gather.15.cloned.1.call-start = ((), (), s32[]{:S(2)}) async-start(), calls=%async_computation.4 | async-start | bytes 4718592 | tf_op jit(solution)/shard_map/all_gather | solution.py:10
  179.3 32.7 %collective-permute-start.2 = (bf16[512,768]{1,0:T(8,128)(2,1)}, bf16[512,768]{1,0:T(8,128)(2,1)S(1)}, u32[]{:S(2)}, u32[]{:S(2)}) collective-permute-start(bf16[512,768]{1,0:T(8,128)(2,1)} %copy-done.6), channel_id=1, source_target_pairs={{0,8},{8,16},{16,24},{24,32},{32,40},{40,48},{48,56},{56,64},{64,7... | collective-permute-start | bytes 2359304 | tf_op jit(solution)/shard_map/ppermute | solution.py:15
  213.9 2.4 copy-start.8
  328.7 3.1 copy-start.9
  514.2 3.3 copy-start.5
  691.9 3.4 copy-start.7
  869.5 3.2 copy-start.1
  869.5 3.2 copy-start.2
  869.5 3.2 copy-start.3
Sparse Core Ops, SparseCore 0:
  142.8 181.4 all-gather.8
  327.4 182.3 all-gather.10
  512.8 174.6 all-gather.12
  690.4 174.6 all-gather.14
